TPU v7x, 32 devices: a whole 2x2x4 slice. The times are simulated.
32 devices in a mesh: group: 4 (over y, core), shard: 8 (over z, x).
Axes of the slice: x: 2, y: 2, z: 4, core: 2. Of those that a mesh axis runs over, the one named last changes fastest.
Arguments:
- queries: bfloat16 [512, 32, 128], P(('group', 'shard')), may hold values from -12 to 12
- passages: bfloat16 [2048, 64, 128], P(('group', 'shard')), may hold values from -4 to 4
- candidates: int32 [512, 160], P(('group', 'shard')), may hold values from 0 to 2047, as said below
- passage_slot: int32 [2048], replicated, may hold values from 0 to 2047, as said below
Outputs:
- scores: float32 [512, 160], P(('group', 'shard'))
Inputs may be any that keep to these rules, and one draw needn't show every extreme that they name: `passage_slot`: every storage row is named by exactly one passage id. `candidates`: candidates k * 20 to (k + 1) * 20 - 1 of a query, for k < 8, all lie in the storage rows of one device, rows d * 64 to (d + 1) * 64 - 1 of device d counted group-major. Over the 16 queries of one device, at most 12 such groups name any one device, and some devices are named exactly 12 times by the queries of every device.
All inputs are finite; a program needn't handle non-finite values.
Results may differ from a plain program's by a relative error of at most 0.0003.
Values may be sent and summed in bfloat16 or wider, within the bound.
No kernel may reach another device: no remote copies, remote signals or barrier semaphores. Data moves between devices by JAX's collectives and lax.ppermute only.
A program may use at most 64 MiB of HBM per device.

v0:
```python
import jax
import jax.numpy as jnp
from jax import lax
from jax.sharding import PartitionSpec as P

PER_VISIT = 20


def score_visits(query_rows, local_rows, passages):
    item_count, peer_width, qtok_count, dim_count = query_rows.shape
    slot_count, ptok_count = (passages.shape[0], passages.shape[1])
    visit_total = item_count * peer_width
    block_size = 16
    store_flat = passages.reshape(slot_count * ptok_count, dim_count)
    query_blocks = query_rows.reshape(visit_total // block_size, block_size, qtok_count, dim_count)
    row_blocks = local_rows.reshape(visit_total // block_size, block_size, local_rows.shape[2])
    slot_ids = jnp.arange(slot_count, dtype=jnp.int32)

    def one_block(pieces):
        query_block, row_block = pieces
        similarity = jnp.einsum(
            "vqd,sd->vqs", query_block, store_flat, preferred_element_type=jnp.float32
        )
        best_match = jnp.max(
            similarity.reshape(block_size, qtok_count, slot_count, ptok_count), axis=3
        )
        passage_score = jnp.sum(best_match, axis=1) / qtok_count
        picker = (row_block[:, :, None] == slot_ids[None, None, :]).astype(jnp.float32)
        return jnp.sum(picker * passage_score[:, None, :], axis=2)

    visit_scores = lax.map(one_block, (query_blocks, row_blocks))
    visit_scores = visit_scores.reshape(item_count, peer_width, local_rows.shape[2])
    return lax.all_to_all(visit_scores, ("group", "shard"), split_axis=1, concat_axis=1, tiled=True)


def local(queries, passages, candidates, passage_slot):
    peer_count = lax.axis_size(("group", "shard"))
    query_count, cand_count = candidates.shape
    slot_count = passages.shape[0]
    spread_count = cand_count // PER_VISIT
    capacity = 3 * query_count * spread_count // peer_count
    visit_count = query_count * spread_count
    storage = passage_slot[candidates].reshape(visit_count, PER_VISIT)
    target = storage[:, 0] // slot_count
    local_rows = storage % slot_count
    matches = (target[:, None] == jnp.arange(peer_count, dtype=jnp.int32)[None, :]).astype(
        jnp.int32
    )
    before = jnp.cumsum(matches, axis=0) - matches
    rank_in = jnp.sum(before * matches, axis=1)
    position = rank_in * peer_count + target
    holder = (
        jnp.zeros((capacity * peer_count,), jnp.int32)
        .at[position]
        .set(jnp.arange(visit_count, dtype=jnp.int32))
    )
    send_local = local_rows[holder].reshape(capacity, peer_count, PER_VISIT)
    query_local = holder // spread_count
    everyone = lax.all_gather(queries, ("group", "shard"), axis=0, tiled=True)
    query_global = (lax.axis_index(("group", "shard")) * query_count + query_local).reshape(
        capacity, peer_count
    )
    wanted = lax.all_to_all(
        query_global, ("group", "shard"), split_axis=1, concat_axis=1, tiled=True
    )
    local_block = lax.all_to_all(
        send_local, ("group", "shard"), split_axis=1, concat_axis=1, tiled=True
    )
    returned = score_visits(everyone[wanted], local_block, passages)
    flat_scores = returned.reshape(capacity * peer_count, PER_VISIT)[position]
    return flat_scores.reshape(query_count, cand_count)


def solution(mesh):
    return jax.shard_map(
        local,
        mesh=mesh,
        in_specs=(
            P(("group", "shard"), None, None),
            P(("group", "shard"), None, None),
            P(("group", "shard"), None),
            P(),
        ),
        out_specs=P(("group", "shard"), None),
        check_vma=False,
    )
```

profile of v0, /device:TPU:0, one launch (start us, length us, event | category | flops | bytes accessed | tf_op | source)
XLA Modules:
  0.0 248.6 jit_solution(6655536599872342939)
XLA Ops:
  6.5 0.7 all-gather.2.cloned.1.call-update
  7.3 0.7 compare_select_fusion.2
  8.1 13.6 %gather_fusion = s32[2560]{0:T(1024)S(1)} fusion(s32[2048]{0:T(1024)S(1)} %copy-done, s32[3072]{0:T(1024)S(1)} %pad_clamp_fusion), kind=kCustom, calls=%fused_computation | custom fusion | bytes 30720 | tf_op jit(solution)/shard_map/gather | solution.py:43
  22.7 1.0 scatter_custom_fusion
  23.7 0.7 copy.19
  24.4 7.3 %all-to-all-start.1 = ((s32[12,32,1]{0,2,1:T(1,128)}), s32[12,32,1]{0,2,1:T(1,128)S(1)}, u32[]{:S(2)}, u32[]{:S(2)}) async-start(s32[12,32,1]{0,2,1:T(1,128)} %copy.19), calls=%async_computation.1 | async-start | bytes 32768 | tf_op jit(solution)/shard_map/all_to_all | solution.py:63
  31.8 1.1 gather_fusion.1
  33.1 0.8 reshape.105
  33.9 5.0 %all-to-all-done.1 = s32[12,32,1]{0,2,1:T(1,128)S(1)} async-done(((s32[12,32,1]{0,2,1:T(1,128)}), s32[12,32,1]{0,2,1:T(1,128)S(1)}, u32[]{:S(2)}, u32[]{:S(2)}) %all-to-all-start.1) | async-done | bytes 1568 | tf_op jit(solution)/shard_map/all_to_all | solution.py:63
  38.8 2.5 %all-to-all-start = ((s32[32,1,240]{2,1,0:T(1,128)}), s32[32,1,240]{2,1,0:T(1,128)S(1)}, u32[]{:S(2)}, u32[]{:S(2)}) async-start(s32[32,1,240]{2,1,0:T(1,128)} %reshape.105), calls=%async_computation | async-start | bytes 65536 | tf_op jit(solution)/shard_map/all_to_all | solution.py:66
  41.6 7.0 %all-to-all-done = s32[32,1,240]{2,1,0:T(1,128)S(1)} async-done(((s32[32,1,240]{2,1,0:T(1,128)}), s32[32,1,240]{2,1,0:T(1,128)S(1)}, u32[]{:S(2)}, u32[]{:S(2)}) %all-to-all-start) | async-done | bytes 30752 | tf_op jit(solution)/shard_map/all_to_all | solution.py:66
  48.6 0.5 broadcast.107
  49.1 0.7 reduce.4
  50.1 24.7 %all-gather.2.cloned.1.call-done = bf16[512,32,128]{2,1,0:T(8,128)(2,1)} async-done(((bf16[16,32,128]{2,1,0:T(8,128)(2,1)}), bf16[512,32,128]{2,1,0:T(8,128)(2,1)}) %all-gather.2.cloned.1.call-update) | async-done | bytes 4194320 | tf_op jit(solution)/shard_map/all_gather | solution.py:59
  74.8 4.9 %gather_fusion.2 = bf16[384,32,128]{2,1,0:T(8,128)(2,1)} fusion(bf16[512,32,128]{2,1,0:T(8,128)(2,1)} %all-gather.2.cloned.1.call-done, s32[1024]{0:T(1024)S(1)} %pad_clamp_fusion.2), kind=kCustom, calls=%fused_computation.2 | custom fusion | bytes 6292992 | tf_op jit(solution)/shard_map/gather | solution.py:69
  79.7 147.7 %while.11 = (s32[]{:T(128)}, f32[24,16,20]{2,1,0:T(8,128)S(1)}, s32[24,16,20]{2,1,0:T(8,128)S(1)}, bf16[24,16,32,128]{3,2,1,0:T(8,128)(2,1)}, bf16[4096,128]{1,0:T(8,128)(2,1)S(1)}, /*index=5*/s32[]{:T(128)}, f32[]{:T(128)}) while((s32[]{:T(128)}, f32[24,16,20]{2,1,0:T(8,128)S(1)}, s32[24,16,20]{2,1,0:T(8,128)S(1)}, ...), condition=%wide.region_7.8_spmd.clone, body=%wide.region_3.7_spmd.clone.sunk | while | flops 539029184 | bytes 1484901 | solution.py:31
  79.8 5.5 %convolution_reduce_fusion.2 = f32[16,32,64]{1,2,0:T(8,128)S(1)} fusion(bf16[64,64,128,1]{2,1,0,3:T(8,128)(2,1)S(1)} %bitcast.53, bf16[24,16,32,128]{3,2,1,0:T(8,128)(2,1)} %get-tuple-element.110, s32[]{:T(128)S(6)} %copy.35), kind=kOutput, calls=%fused_computation.6.clone.1 | convolution fusion | flops 538935296 | bytes 1310724 | tf_op jit(solution)/shard_map/while/body/eval_jaxpr/vqd,sd->vqs/dot_general | solution.py:21
  85.4 0.2 reduce_sum.35
  86.0 5.5 %convolution_reduce_fusion.2 = f32[16,32,64]{1,2,0:T(8,128)S(1)} fusion(bf16[64,64,128,1]{2,1,0,3:T(8,128)(2,1)S(1)} %bitcast.53, bf16[24,16,32,128]{3,2,1,0:T(8,128)(2,1)} %get-tuple-element.110, s32[]{:T(128)S(6)} %copy.35), kind=kOutput, calls=%fused_computation.6.clone.1 | convolution fusion | flops 538935296 | bytes 1310724 | tf_op jit(solution)/shard_map/while/body/eval_jaxpr/vqd,sd->vqs/dot_general | solution.py:21
  92.1 5.5 %convolution_reduce_fusion.2 = f32[16,32,64]{1,2,0:T(8,128)S(1)} fusion(bf16[64,64,128,1]{2,1,0,3:T(8,128)(2,1)S(1)} %bitcast.53, bf16[24,16,32,128]{3,2,1,0:T(8,128)(2,1)} %get-tuple-element.110, s32[]{:T(128)S(6)} %copy.35), kind=kOutput, calls=%fused_computation.6.clone.1 | convolution fusion | flops 538935296 | bytes 1310724 | tf_op jit(solution)/shard_map/while/body/eval_jaxpr/vqd,sd->vqs/dot_general | solution.py:21
  98.3 5.5 %convolution_reduce_fusion.2 = f32[16,32,64]{1,2,0:T(8,128)S(1)} fusion(bf16[64,64,128,1]{2,1,0,3:T(8,128)(2,1)S(1)} %bitcast.53, bf16[24,16,32,128]{3,2,1,0:T(8,128)(2,1)} %get-tuple-element.110, s32[]{:T(128)S(6)} %copy.35), kind=kOutput, calls=%fused_computation.6.clone.1 | convolution fusion | flops 538935296 | bytes 1310724 | tf_op jit(solution)/shard_map/while/body/eval_jaxpr/vqd,sd->vqs/dot_general | solution.py:21
  104.5 5.5 %convolution_reduce_fusion.2 = f32[16,32,64]{1,2,0:T(8,128)S(1)} fusion(bf16[64,64,128,1]{2,1,0,3:T(8,128)(2,1)S(1)} %bitcast.53, bf16[24,16,32,128]{3,2,1,0:T(8,128)(2,1)} %get-tuple-element.110, s32[]{:T(128)S(6)} %copy.35), kind=kOutput, calls=%fused_computation.6.clone.1 | convolution fusion | flops 538935296 | bytes 1310724 | tf_op jit(solution)/shard_map/while/body/eval_jaxpr/vqd,sd->vqs/dot_general | solution.py:21
  110.6 5.5 %convolution_reduce_fusion.2 = f32[16,32,64]{1,2,0:T(8,128)S(1)} fusion(bf16[64,64,128,1]{2,1,0,3:T(8,128)(2,1)S(1)} %bitcast.53, bf16[24,16,32,128]{3,2,1,0:T(8,128)(2,1)} %get-tuple-element.110, s32[]{:T(128)S(6)} %copy.35), kind=kOutput, calls=%fused_computation.6.clone.1 | convolution fusion | flops 538935296 | bytes 1310724 | tf_op jit(solution)/shard_map/while/body/eval_jaxpr/vqd,sd->vqs/dot_general | solution.py:21
  116.8 5.5 %convolution_reduce_fusion.2 = f32[16,32,64]{1,2,0:T(8,128)S(1)} fusion(bf16[64,64,128,1]{2,1,0,3:T(8,128)(2,1)S(1)} %bitcast.53, bf16[24,16,32,128]{3,2,1,0:T(8,128)(2,1)} %get-tuple-element.110, s32[]{:T(128)S(6)} %copy.35), kind=kOutput, calls=%fused_computation.6.clone.1 | convolution fusion | flops 538935296 | bytes 1310724 | tf_op jit(solution)/shard_map/while/body/eval_jaxpr/vqd,sd->vqs/dot_general | solution.py:21
  122.9 5.5 %convolution_reduce_fusion.2 = f32[16,32,64]{1,2,0:T(8,128)S(1)} fusion(bf16[64,64,128,1]{2,1,0,3:T(8,128)(2,1)S(1)} %bitcast.53, bf16[24,16,32,128]{3,2,1,0:T(8,128)(2,1)} %get-tuple-element.110, s32[]{:T(128)S(6)} %copy.35), kind=kOutput, calls=%fused_computation.6.clone.1 | convolution fusion | flops 538935296 | bytes 1310724 | tf_op jit(solution)/shard_map/while/body/eval_jaxpr/vqd,sd->vqs/dot_general | solution.py:21
  129.1 5.5 %convolution_reduce_fusion.2 = f32[16,32,64]{1,2,0:T(8,128)S(1)} fusion(bf16[64,64,128,1]{2,1,0,3:T(8,128)(2,1)S(1)} %bitcast.53, bf16[24,16,32,128]{3,2,1,0:T(8,128)(2,1)} %get-tuple-element.110, s32[]{:T(128)S(6)} %copy.35), kind=kOutput, calls=%fused_computation.6.clone.1 | convolution fusion | flops 538935296 | bytes 1310724 | tf_op jit(solution)/shard_map/while/body/eval_jaxpr/vqd,sd->vqs/dot_general | solution.py:21
  135.2 5.5 %convolution_reduce_fusion.2 = f32[16,32,64]{1,2,0:T(8,128)S(1)} fusion(bf16[64,64,128,1]{2,1,0,3:T(8,128)(2,1)S(1)} %bitcast.53, bf16[24,16,32,128]{3,2,1,0:T(8,128)(2,1)} %get-tuple-element.110, s32[]{:T(128)S(6)} %copy.35), kind=kOutput, calls=%fused_computation.6.clone.1 | convolution fusion | flops 538935296 | bytes 1310724 | tf_op jit(solution)/shard_map/while/body/eval_jaxpr/vqd,sd->vqs/dot_general | solution.py:21
  141.4 5.5 %convolution_reduce_fusion.2 = f32[16,32,64]{1,2,0:T(8,128)S(1)} fusion(bf16[64,64,128,1]{2,1,0,3:T(8,128)(2,1)S(1)} %bitcast.53, bf16[24,16,32,128]{3,2,1,0:T(8,128)(2,1)} %get-tuple-element.110, s32[]{:T(128)S(6)} %copy.35), kind=kOutput, calls=%fused_computation.6.clone.1 | convolution fusion | flops 538935296 | bytes 1310724 | tf_op jit(solution)/shard_map/while/body/eval_jaxpr/vqd,sd->vqs/dot_general | solution.py:21
  147.5 5.5 %convolution_reduce_fusion.2 = f32[16,32,64]{1,2,0:T(8,128)S(1)} fusion(bf16[64,64,128,1]{2,1,0,3:T(8,128)(2,1)S(1)} %bitcast.53, bf16[24,16,32,128]{3,2,1,0:T(8,128)(2,1)} %get-tuple-element.110, s32[]{:T(128)S(6)} %copy.35), kind=kOutput, calls=%fused_computation.6.clone.1 | convolution fusion | flops 538935296 | bytes 1310724 | tf_op jit(solution)/shard_map/while/body/eval_jaxpr/vqd,sd->vqs/dot_general | solution.py:21
  153.7 5.5 %convolution_reduce_fusion.2 = f32[16,32,64]{1,2,0:T(8,128)S(1)} fusion(bf16[64,64,128,1]{2,1,0,3:T(8,128)(2,1)S(1)} %bitcast.53, bf16[24,16,32,128]{3,2,1,0:T(8,128)(2,1)} %get-tuple-element.110, s32[]{:T(128)S(6)} %copy.35), kind=kOutput, calls=%fused_computation.6.clone.1 | convolution fusion | flops 538935296 | bytes 1310724 | tf_op jit(solution)/shard_map/while/body/eval_jaxpr/vqd,sd->vqs/dot_general | solution.py:21
  159.9 5.5 %convolution_reduce_fusion.2 = f32[16,32,64]{1,2,0:T(8,128)S(1)} fusion(bf16[64,64,128,1]{2,1,0,3:T(8,128)(2,1)S(1)} %bitcast.53, bf16[24,16,32,128]{3,2,1,0:T(8,128)(2,1)} %get-tuple-element.110, s32[]{:T(128)S(6)} %copy.35), kind=kOutput, calls=%fused_computation.6.clone.1 | convolution fusion | flops 538935296 | bytes 1310724 | tf_op jit(solution)/shard_map/while/body/eval_jaxpr/vqd,sd->vqs/dot_general | solution.py:21
  166.0 5.5 %convolution_reduce_fusion.2 = f32[16,32,64]{1,2,0:T(8,128)S(1)} fusion(bf16[64,64,128,1]{2,1,0,3:T(8,128)(2,1)S(1)} %bitcast.53, bf16[24,16,32,128]{3,2,1,0:T(8,128)(2,1)} %get-tuple-element.110, s32[]{:T(128)S(6)} %copy.35), kind=kOutput, calls=%fused_computation.6.clone.1 | convolution fusion | flops 538935296 | bytes 1310724 | tf_op jit(solution)/shard_map/while/body/eval_jaxpr/vqd,sd->vqs/dot_general | solution.py:21
  172.2 5.5 %convolution_reduce_fusion.2 = f32[16,32,64]{1,2,0:T(8,128)S(1)} fusion(bf16[64,64,128,1]{2,1,0,3:T(8,128)(2,1)S(1)} %bitcast.53, bf16[24,16,32,128]{3,2,1,0:T(8,128)(2,1)} %get-tuple-element.110, s32[]{:T(128)S(6)} %copy.35), kind=kOutput, calls=%fused_computation.6.clone.1 | convolution fusion | flops 538935296 | bytes 1310724 | tf_op jit(solution)/shard_map/while/body/eval_jaxpr/vqd,sd->vqs/dot_general | solution.py:21
  178.3 5.5 %convolution_reduce_fusion.2 = f32[16,32,64]{1,2,0:T(8,128)S(1)} fusion(bf16[64,64,128,1]{2,1,0,3:T(8,128)(2,1)S(1)} %bitcast.53, bf16[24,16,32,128]{3,2,1,0:T(8,128)(2,1)} %get-tuple-element.110, s32[]{:T(128)S(6)} %copy.35), kind=kOutput, calls=%fused_computation.6.clone.1 | convolution fusion | flops 538935296 | bytes 1310724 | tf_op jit(solution)/shard_map/while/body/eval_jaxpr/vqd,sd->vqs/dot_general | solution.py:21
  184.5 5.5 %convolution_reduce_fusion.2 = f32[16,32,64]{1,2,0:T(8,128)S(1)} fusion(bf16[64,64,128,1]{2,1,0,3:T(8,128)(2,1)S(1)} %bitcast.53, bf16[24,16,32,128]{3,2,1,0:T(8,128)(2,1)} %get-tuple-element.110, s32[]{:T(128)S(6)} %copy.35), kind=kOutput, calls=%fused_computation.6.clone.1 | convolution fusion | flops 538935296 | bytes 1310724 | tf_op jit(solution)/shard_map/while/body/eval_jaxpr/vqd,sd->vqs/dot_general | solution.py:21
  190.6 5.5 %convolution_reduce_fusion.2 = f32[16,32,64]{1,2,0:T(8,128)S(1)} fusion(bf16[64,64,128,1]{2,1,0,3:T(8,128)(2,1)S(1)} %bitcast.53, bf16[24,16,32,128]{3,2,1,0:T(8,128)(2,1)} %get-tuple-element.110, s32[]{:T(128)S(6)} %copy.35), kind=kOutput, calls=%fused_computation.6.clone.1 | convolution fusion | flops 538935296 | bytes 1310724 | tf_op jit(solution)/shard_map/while/body/eval_jaxpr/vqd,sd->vqs/dot_general | solution.py:21
  196.8 5.5 %convolution_reduce_fusion.2 = f32[16,32,64]{1,2,0:T(8,128)S(1)} fusion(bf16[64,64,128,1]{2,1,0,3:T(8,128)(2,1)S(1)} %bitcast.53, bf16[24,16,32,128]{3,2,1,0:T(8,128)(2,1)} %get-tuple-element.110, s32[]{:T(128)S(6)} %copy.35), kind=kOutput, calls=%fused_computation.6.clone.1 | convolution fusion | flops 538935296 | bytes 1310724 | tf_op jit(solution)/shard_map/while/body/eval_jaxpr/vqd,sd->vqs/dot_general | solution.py:21
  202.9 5.5 %convolution_reduce_fusion.2 = f32[16,32,64]{1,2,0:T(8,128)S(1)} fusion(bf16[64,64,128,1]{2,1,0,3:T(8,128)(2,1)S(1)} %bitcast.53, bf16[24,16,32,128]{3,2,1,0:T(8,128)(2,1)} %get-tuple-element.110, s32[]{:T(128)S(6)} %copy.35), kind=kOutput, calls=%fused_computation.6.clone.1 | convolution fusion | flops 538935296 | bytes 1310724 | tf_op jit(solution)/shard_map/while/body/eval_jaxpr/vqd,sd->vqs/dot_general | solution.py:21
  209.1 5.5 %convolution_reduce_fusion.2 = f32[16,32,64]{1,2,0:T(8,128)S(1)} fusion(bf16[64,64,128,1]{2,1,0,3:T(8,128)(2,1)S(1)} %bitcast.53, bf16[24,16,32,128]{3,2,1,0:T(8,128)(2,1)} %get-tuple-element.110, s32[]{:T(128)S(6)} %copy.35), kind=kOutput, calls=%fused_computation.6.clone.1 | convolution fusion | flops 538935296 | bytes 1310724 | tf_op jit(solution)/shard_map/while/body/eval_jaxpr/vqd,sd->vqs/dot_general | solution.py:21
  215.3 5.5 %convolution_reduce_fusion.2 = f32[16,32,64]{1,2,0:T(8,128)S(1)} fusion(bf16[64,64,128,1]{2,1,0,3:T(8,128)(2,1)S(1)} %bitcast.53, bf16[24,16,32,128]{3,2,1,0:T(8,128)(2,1)} %get-tuple-element.110, s32[]{:T(128)S(6)} %copy.35), kind=kOutput, calls=%fused_computation.6.clone.1 | convolution fusion | flops 538935296 | bytes 1310724 | tf_op jit(solution)/shard_map/while/body/eval_jaxpr/vqd,sd->vqs/dot_general | solution.py:21
  221.4 5.5 %convolution_reduce_fusion.2 = f32[16,32,64]{1,2,0:T(8,128)S(1)} fusion(bf16[64,64,128,1]{2,1,0,3:T(8,128)(2,1)S(1)} %bitcast.53, bf16[24,16,32,128]{3,2,1,0:T(8,128)(2,1)} %get-tuple-element.110, s32[]{:T(128)S(6)} %copy.35), kind=kOutput, calls=%fused_computation.6.clone.1 | convolution fusion | flops 538935296 | bytes 1310724 | tf_op jit(solution)/shard_map/while/body/eval_jaxpr/vqd,sd->vqs/dot_general | solution.py:21
  227.6 0.8 reshape.107
  228.4 3.4 %all-to-all-start.2 = ((f32[32,1,240]{2,1,0:T(1,128)}), f32[32,1,240]{2,1,0:T(1,128)S(1)}, u32[]{:S(2)}, u32[]{:S(2)}) async-start(f32[32,1,240]{2,1,0:T(1,128)} %reshape.107), calls=%async_computation.2 | async-start | bytes 65536 | tf_op jit(solution)/shard_map/all_to_all | solution.py:33
  231.8 7.2 %all-to-all-done.2 = f32[32,1,240]{2,1,0:T(1,128)S(1)} async-done(((f32[32,1,240]{2,1,0:T(1,128)}), f32[32,1,240]{2,1,0:T(1,128)S(1)}, u32[]{:S(2)}, u32[]{:S(2)}) %all-to-all-start.2) | async-done | bytes 30752 | tf_op jit(solution)/shard_map/all_to_all | solution.py:33
  239.0 0.5 broadcast.108
  239.5 0.7 reduce.5
  240.4 0.6 gather_fusion.3
  241.1 0.7 reshape.52
  (199 shorter events, 15.9 us)
Async XLA Ops:
  6.5 1.5 copy-start
  6.5 68.3 %all-gather.2.cloned.1.call-start = ((), (), s32[]{:S(2)}) async-start(), calls=%async_computation.3 | async-start | bytes 4325376 | tf_op jit(solution)/shard_map/all_gather | solution.py:59
  24.4 14.4 %all-to-all-start.1 = ((s32[12,32,1]{0,2,1:T(1,128)}), s32[12,32,1]{0,2,1:T(1,128)S(1)}, u32[]{:S(2)}, u32[]{:S(2)}) async-start(s32[12,32,1]{0,2,1:T(1,128)} %copy.19), calls=%async_computation.1 | async-start | bytes 32768 | tf_op jit(solution)/shard_map/all_to_all | solution.py:63
  38.8 9.8 %all-to-all-start = ((s32[32,1,240]{2,1,0:T(1,128)}), s32[32,1,240]{2,1,0:T(1,128)S(1)}, u32[]{:S(2)}, u32[]{:S(2)}) async-start(s32[32,1,240]{2,1,0:T(1,128)} %reshape.105), calls=%async_computation | async-start | bytes 65536 | tf_op jit(solution)/shard_map/all_to_all | solution.py:66
  50.1 29.7 %copy-start.1 = (bf16[64,64,128]{2,1,0:T(8,128)(2,1)S(1)}, bf16[64,64,128]{2,1,0:T(8,128)(2,1)}, u32[]{:S(2)}) copy-start(bf16[64,64,128]{2,1,0:T(8,128)(2,1)} %param.7) | copy-start | bytes 3145732
  228.4 10.6 %all-to-all-start.2 = ((f32[32,1,240]{2,1,0:T(1,128)}), f32[32,1,240]{2,1,0:T(1,128)S(1)}, u32[]{:S(2)}, u32[]{:S(2)}) async-start(f32[32,1,240]{2,1,0:T(1,128)} %reshape.107), calls=%async_computation.2 | async-start | bytes 65536 | tf_op jit(solution)/shard_map/all_to_all | solution.py:33
Sparse Core Ops, SparseCore 0:
  10.3 64.4 all-gather.1
where the time goes:
time: 249 us
  matrix products  133 us (53%)
  waiting for transfers between devices  44.6 us (18%)
  local copies, waits for them, and re-layouts  30.6 us (12%)
  between operations  13.6 us (5%)
  starting transfers between devices  13.3 us (5%)
  other arithmetic  12.9 us (5%)
    dot_general x24, matrix products, one_block(): jnp.einsum('vqd,sd->vqs', query_block, store_flat, preferred_element_type...  133 us
    all_gather x1, waiting for transfers between devices, local(): everyone = lax.all_gather(queries, ('group', 'shard'), axis=0, tiled=True)  24.7 us
    gather x1, local copies, waits for them, and re-layouts, local(): storage = passage_slot[candidates].reshape(visit_count, PER_VISIT)  13.6 us
    all_to_all x1, starting transfers between devices, local(): lax.all_to_all(query_global, ('group', 'shard'), split_axis=1, concat_axi...  7.33 us
    all_to_all x1, waiting for transfers between devices, score_visits(): lax.all_to_all(visit_scores, ('group', 'shard'), split_axis=1, concat_axi...  7.18 us
    all_to_all x1, waiting for transfers between devices, local(): lax.all_to_all(send_local, ('group', 'shard'), split_axis=1, concat_axis=...  7.04 us
    reduce_sum x24, other arithmetic, one_block(): passage_score = jnp.sum(best_match, axis=1) / qtok_count  5.03 us
    all_to_all x1, waiting for transfers between devices, local(): lax.all_to_all(query_global, ('group', 'shard'), split_axis=1, concat_axi...  4.98 us
  transfers between devices with their start and end apart: 4, of which 4 were waited for; matrix products, arithmetic and copies ran while one was open for 8% of the time, Pallas kernels for 0%

commit v1 on v0

--- a/solution.py
+++ b/solution.py
@@ -60,9 +60,14 @@
     query_global = (lax.axis_index(("group", "shard")) * query_count + query_local).reshape(
         capacity, peer_count
     )
-    wanted = lax.all_to_all(
-        query_global, ("group", "shard"), split_axis=1, concat_axis=1, tiled=True
-    )
+
+    def _raise_runs(block_in, dev_axis):
+        arr_out = lax.all_to_all(
+            jnp.stack(jnp.split(block_in, lax.axis_size(dev_axis), axis=1)), dev_axis, 0, 0
+        )
+        return jnp.concatenate(arr_out, axis=1)
+
+    wanted = _raise_runs(query_global, ("group", "shard"))
     local_block = lax.all_to_all(
         send_local, ("group", "shard"), split_axis=1, concat_axis=1, tiled=True
     )

time: 249 us -> 249 us (level)
  waiting for transfers between devices: 44.6 us -> 21.2 us
  local copies, waits for them, and re-layouts: 30.6 us -> 46.7 us
  blocking collectives: 0 us -> 10.4 us
  starting transfers between devices: 13.3 us -> 9.87 us
    all_gather x1, waiting for transfers between devices: 24.7 us -> 8.22 us  [local(): everyone = lax.all_gather(queries, ('group', 'shard'), axis=0, tiled=True)]
    unnamed x8 -> x39, local copies, waits for them, and re-layouts: 1.83 us -> 17.1 us
    all_to_all x0 -> x1, blocking collectives: none -> 10.4 us  [score_visits(): lax.all_to_all(visit_scores, ('group', 'shard'), split_axis=1, concat_axi...]
    all_to_all x2 -> x1, waiting for transfers between devices: 12.2 us -> 4.98 us  [_raise_runs(): lax.all_to_all(jnp.stack(jnp.split(block_in, lax.axis_size(dev_axis), axi...]
    all_to_all x2 -> x1, starting transfers between devices: 10.7 us -> 7.33 us  [_raise_runs(): lax.all_to_all(jnp.stack(jnp.split(block_in, lax.axis_size(dev_axis), axi...]
  transfers between devices with their start and end apart: 4 -> 3, of which waited for: 4 -> 3; matrix products, arithmetic and copies ran while one was open for 8% -> 15% of each run, Pallas kernels for 0% -> 0%
where the time goes in v1:
time: 249 us
  matrix products  133 us (53%)
  local copies, waits for them, and re-layouts  46.7 us (19%)
  waiting for transfers between devices  21.2 us (9%)
  between operations  13.6 us (5%)
  other arithmetic  12.9 us (5%)
  blocking collectives  10.4 us (4%)
  starting transfers between devices  9.87 us (4%)
    dot_general x24, matrix products, one_block(): jnp.einsum('vqd,sd->vqs', query_block, store_flat, preferred_element_type...  133 us
    unnamed x39, local copies, waits for them, and re-layouts  17.1 us
    gather x1, local copies, waits for them, and re-layouts, local(): storage = passage_slot[candidates].reshape(visit_count, PER_VISIT)  13.6 us
    all_to_all x1, blocking collectives, score_visits(): lax.all_to_all(visit_scores, ('group', 'shard'), split_axis=1, concat_axi...  10.4 us
    all_gather x1, waiting for transfers between devices, local(): everyone = lax.all_gather(queries, ('group', 'shard'), axis=0, tiled=True)  8.22 us
    all_to_all x1, starting transfers between devices, _raise_runs(): lax.all_to_all(jnp.stack(jnp.split(block_in, lax.axis_size(dev_axis), axi...  7.33 us
    all_to_all x1, waiting for transfers between devices, local(): lax.all_to_all(send_local, ('group', 'shard'), split_axis=1, concat_axis=...  7.25 us
    reduce_sum x24, other arithmetic, one_block(): passage_score = jnp.sum(best_match, axis=1) / qtok_count  5.03 us
  transfers between devices with their start and end apart: 3, of which 3 were waited for; matrix products, arithmetic and copies ran while one was open for 15% of the time, Pallas kernels for 0%

profile of v1, /device:TPU:0, one launch (start us, length us, event | category | flops | bytes accessed | tf_op | source)
XLA Modules:
  0.0 248.6 jit_solution(3510382068403330313)
XLA Ops:
  6.5 0.7 all-gather.2.cloned.1.call-update
  7.3 0.7 compare_select_fusion.2
  8.1 13.6 %gather_fusion = s32[2560]{0:T(1024)S(1)} fusion(s32[2048]{0:T(1024)S(1)} %copy-done, s32[3072]{0:T(1024)S(1)} %pad_clamp_fusion), kind=kCustom, calls=%fused_computation | custom fusion | bytes 30720 | tf_op jit(solution)/shard_map/gather | solution.py:43
  22.7 1.0 scatter_custom_fusion
  24.2 0.5 slice_reduce_fusion
  24.7 0.5 constant_dynamic-update-slice_fusion.31
  25.7 0.5 constant_dynamic-update-slice_fusion.29
  26.2 0.5 constant_dynamic-update-slice_fusion.28
  26.7 0.5 constant_dynamic-update-slice_fusion.27
  27.2 0.5 constant_dynamic-update-slice_fusion.26
  41.1 7.3 %all-to-all-start.1 = ((s32[32,12,1]{1,2,0:T(1,128)}), s32[32,12,1]{1,2,0:T(1,128)S(1)}, u32[]{:S(2)}, u32[]{:S(2)}) async-start(s32[32,12,1]{1,2,0:T(1,128)} %constant_dynamic-update-slice_fusion), calls=%async_computation.1 | async-start | bytes 32768 | tf_op jit(solution)/shard_map/all_to_all | solution.py:65
  48.5 1.1 gather_fusion.1
  49.7 0.8 reshape.142
  50.5 5.0 %all-to-all-done.1 = s32[32,12,1]{1,2,0:T(1,128)S(1)} async-done(((s32[32,12,1]{1,2,0:T(1,128)}), s32[32,12,1]{1,2,0:T(1,128)S(1)}, u32[]{:S(2)}, u32[]{:S(2)}) %all-to-all-start.1) | async-done | bytes 1568 | tf_op jit(solution)/shard_map/all_to_all | solution.py:65
  55.5 2.5 %all-to-all-start = ((s32[32,1,240]{2,1,0:T(1,128)}), s32[32,1,240]{2,1,0:T(1,128)S(1)}, u32[]{:S(2)}, u32[]{:S(2)}) async-start(s32[32,1,240]{2,1,0:T(1,128)} %reshape.142), calls=%async_computation | async-start | bytes 65536 | tf_op jit(solution)/shard_map/all_to_all | solution.py:71
  58.2 7.3 %all-to-all-done = s32[32,1,240]{2,1,0:T(1,128)S(1)} async-done(((s32[32,1,240]{2,1,0:T(1,128)}), s32[32,1,240]{2,1,0:T(1,128)S(1)}, u32[]{:S(2)}, u32[]{:S(2)}) %all-to-all-start) | async-done | bytes 30752 | tf_op jit(solution)/shard_map/all_to_all | solution.py:71
  66.0 0.7 reduce.68
  66.9 8.2 %all-gather.2.cloned.1.call-done = bf16[512,32,128]{2,1,0:T(8,128)(2,1)} async-done(((bf16[16,32,128]{2,1,0:T(8,128)(2,1)}), bf16[512,32,128]{2,1,0:T(8,128)(2,1)}) %all-gather.2.cloned.1.call-update) | async-done | bytes 4194320 | tf_op jit(solution)/shard_map/all_gather | solution.py:59
  75.2 4.9 %gather_fusion.2 = bf16[384,32,128]{2,1,0:T(8,128)(2,1)} fusion(bf16[512,32,128]{2,1,0:T(8,128)(2,1)} %all-gather.2.cloned.1.call-done, s32[1024]{0:T(1024)S(1)} %pad_clamp_fusion.2), kind=kCustom, calls=%fused_computation.2 | custom fusion | bytes 6292992 | tf_op jit(solution)/shard_map/gather | solution.py:74
  80.1 148.2 %while.11 = (s32[]{:T(128)}, f32[24,16,20]{2,1,0:T(8,128)S(1)}, s32[24,16,20]{2,1,0:T(8,128)S(1)}, bf16[24,16,32,128]{3,2,1,0:T(8,128)(2,1)}, bf16[4096,128]{1,0:T(8,128)(2,1)S(1)}, /*index=5*/s32[]{:T(128)}, f32[]{:T(128)}) while((s32[]{:T(128)}, f32[24,16,20]{2,1,0:T(8,128)S(1)}, s32[24,16,20]{2,1,0:T(8,128)S(1)}, ...), condition=%wide.region_7.8_spmd.clone, body=%wide.region_3.7_spmd.clone.sunk | while | flops 539029184 | bytes 1485401 | solution.py:31
  80.1 5.6 %convolution_reduce_fusion.2 = f32[16,32,64]{1,2,0:T(8,128)S(1)} fusion(bf16[64,64,128,1]{2,1,0,3:T(8,128)(2,1)S(1)} %bitcast.118, bf16[24,16,32,128]{3,2,1,0:T(8,128)(2,1)} %get-tuple-element.144, s32[]{:T(128)} %get-tuple-element.134), kind=kOutput, calls=%fused_computation.6.clone.1 | convolution fusion | flops 538935296 | bytes 1311232 | tf_op jit(solution)/shard_map/while/body/eval_jaxpr/vqd,sd->vqs/dot_general | solution.py:21
  86.3 5.6 %convolution_reduce_fusion.2 = f32[16,32,64]{1,2,0:T(8,128)S(1)} fusion(bf16[64,64,128,1]{2,1,0,3:T(8,128)(2,1)S(1)} %bitcast.118, bf16[24,16,32,128]{3,2,1,0:T(8,128)(2,1)} %get-tuple-element.144, s32[]{:T(128)} %get-tuple-element.134), kind=kOutput, calls=%fused_computation.6.clone.1 | convolution fusion | flops 538935296 | bytes 1311232 | tf_op jit(solution)/shard_map/while/body/eval_jaxpr/vqd,sd->vqs/dot_general | solution.py:21
  92.4 5.5 %convolution_reduce_fusion.2 = f32[16,32,64]{1,2,0:T(8,128)S(1)} fusion(bf16[64,64,128,1]{2,1,0,3:T(8,128)(2,1)S(1)} %bitcast.118, bf16[24,16,32,128]{3,2,1,0:T(8,128)(2,1)} %get-tuple-element.144, s32[]{:T(128)} %get-tuple-element.134), kind=kOutput, calls=%fused_computation.6.clone.1 | convolution fusion | flops 538935296 | bytes 1311232 | tf_op jit(solution)/shard_map/while/body/eval_jaxpr/vqd,sd->vqs/dot_general | solution.py:21
  98.6 5.5 %convolution_reduce_fusion.2 = f32[16,32,64]{1,2,0:T(8,128)S(1)} fusion(bf16[64,64,128,1]{2,1,0,3:T(8,128)(2,1)S(1)} %bitcast.118, bf16[24,16,32,128]{3,2,1,0:T(8,128)(2,1)} %get-tuple-element.144, s32[]{:T(128)} %get-tuple-element.134), kind=kOutput, calls=%fused_computation.6.clone.1 | convolution fusion | flops 538935296 | bytes 1311232 | tf_op jit(solution)/shard_map/while/body/eval_jaxpr/vqd,sd->vqs/dot_general | solution.py:21
  104.8 5.5 %convolution_reduce_fusion.2 = f32[16,32,64]{1,2,0:T(8,128)S(1)} fusion(bf16[64,64,128,1]{2,1,0,3:T(8,128)(2,1)S(1)} %bitcast.118, bf16[24,16,32,128]{3,2,1,0:T(8,128)(2,1)} %get-tuple-element.144, s32[]{:T(128)} %get-tuple-element.134), kind=kOutput, calls=%fused_computation.6.clone.1 | convolution fusion | flops 538935296 | bytes 1311232 | tf_op jit(solution)/shard_map/while/body/eval_jaxpr/vqd,sd->vqs/dot_general | solution.py:21
  111.0 5.5 %convolution_reduce_fusion.2 = f32[16,32,64]{1,2,0:T(8,128)S(1)} fusion(bf16[64,64,128,1]{2,1,0,3:T(8,128)(2,1)S(1)} %bitcast.118, bf16[24,16,32,128]{3,2,1,0:T(8,128)(2,1)} %get-tuple-element.144, s32[]{:T(128)} %get-tuple-element.134), kind=kOutput, calls=%fused_computation.6.clone.1 | convolution fusion | flops 538935296 | bytes 1311232 | tf_op jit(solution)/shard_map/while/body/eval_jaxpr/vqd,sd->vqs/dot_general | solution.py:21
  117.1 5.5 %convolution_reduce_fusion.2 = f32[16,32,64]{1,2,0:T(8,128)S(1)} fusion(bf16[64,64,128,1]{2,1,0,3:T(8,128)(2,1)S(1)} %bitcast.118, bf16[24,16,32,128]{3,2,1,0:T(8,128)(2,1)} %get-tuple-element.144, s32[]{:T(128)} %get-tuple-element.134), kind=kOutput, calls=%fused_computation.6.clone.1 | convolution fusion | flops 538935296 | bytes 1311232 | tf_op jit(solution)/shard_map/while/body/eval_jaxpr/vqd,sd->vqs/dot_general | solution.py:21
  123.3 5.5 %convolution_reduce_fusion.2 = f32[16,32,64]{1,2,0:T(8,128)S(1)} fusion(bf16[64,64,128,1]{2,1,0,3:T(8,128)(2,1)S(1)} %bitcast.118, bf16[24,16,32,128]{3,2,1,0:T(8,128)(2,1)} %get-tuple-element.144, s32[]{:T(128)} %get-tuple-element.134), kind=kOutput, calls=%fused_computation.6.clone.1 | convolution fusion | flops 538935296 | bytes 1311232 | tf_op jit(solution)/shard_map/while/body/eval_jaxpr/vqd,sd->vqs/dot_general | solution.py:21
  129.5 5.5 %convolution_reduce_fusion.2 = f32[16,32,64]{1,2,0:T(8,128)S(1)} fusion(bf16[64,64,128,1]{2,1,0,3:T(8,128)(2,1)S(1)} %bitcast.118, bf16[24,16,32,128]{3,2,1,0:T(8,128)(2,1)} %get-tuple-element.144, s32[]{:T(128)} %get-tuple-element.134), kind=kOutput, calls=%fused_computation.6.clone.1 | convolution fusion | flops 538935296 | bytes 1311232 | tf_op jit(solution)/shard_map/while/body/eval_jaxpr/vqd,sd->vqs/dot_general | solution.py:21
  135.7 5.5 %convolution_reduce_fusion.2 = f32[16,32,64]{1,2,0:T(8,128)S(1)} fusion(bf16[64,64,128,1]{2,1,0,3:T(8,128)(2,1)S(1)} %bitcast.118, bf16[24,16,32,128]{3,2,1,0:T(8,128)(2,1)} %get-tuple-element.144, s32[]{:T(128)} %get-tuple-element.134), kind=kOutput, calls=%fused_computation.6.clone.1 | convolution fusion | flops 538935296 | bytes 1311232 | tf_op jit(solution)/shard_map/while/body/eval_jaxpr/vqd,sd->vqs/dot_general | solution.py:21
  141.8 5.5 %convolution_reduce_fusion.2 = f32[16,32,64]{1,2,0:T(8,128)S(1)} fusion(bf16[64,64,128,1]{2,1,0,3:T(8,128)(2,1)S(1)} %bitcast.118, bf16[24,16,32,128]{3,2,1,0:T(8,128)(2,1)} %get-tuple-element.144, s32[]{:T(128)} %get-tuple-element.134), kind=kOutput, calls=%fused_computation.6.clone.1 | convolution fusion | flops 538935296 | bytes 1311232 | tf_op jit(solution)/shard_map/while/body/eval_jaxpr/vqd,sd->vqs/dot_general | solution.py:21
  148.0 5.5 %convolution_reduce_fusion.2 = f32[16,32,64]{1,2,0:T(8,128)S(1)} fusion(bf16[64,64,128,1]{2,1,0,3:T(8,128)(2,1)S(1)} %bitcast.118, bf16[24,16,32,128]{3,2,1,0:T(8,128)(2,1)} %get-tuple-element.144, s32[]{:T(128)} %get-tuple-element.134), kind=kOutput, calls=%fused_computation.6.clone.1 | convolution fusion | flops 538935296 | bytes 1311232 | tf_op jit(solution)/shard_map/while/body/eval_jaxpr/vqd,sd->vqs/dot_general | solution.py:21
  154.2 5.5 %convolution_reduce_fusion.2 = f32[16,32,64]{1,2,0:T(8,128)S(1)} fusion(bf16[64,64,128,1]{2,1,0,3:T(8,128)(2,1)S(1)} %bitcast.118, bf16[24,16,32,128]{3,2,1,0:T(8,128)(2,1)} %get-tuple-element.144, s32[]{:T(128)} %get-tuple-element.134), kind=kOutput, calls=%fused_computation.6.clone.1 | convolution fusion | flops 538935296 | bytes 1311232 | tf_op jit(solution)/shard_map/while/body/eval_jaxpr/vqd,sd->vqs/dot_general | solution.py:21
  160.3 5.5 %convolution_reduce_fusion.2 = f32[16,32,64]{1,2,0:T(8,128)S(1)} fusion(bf16[64,64,128,1]{2,1,0,3:T(8,128)(2,1)S(1)} %bitcast.118, bf16[24,16,32,128]{3,2,1,0:T(8,128)(2,1)} %get-tuple-element.144, s32[]{:T(128)} %get-tuple-element.134), kind=kOutput, calls=%fused_computation.6.clone.1 | convolution fusion | flops 538935296 | bytes 1311232 | tf_op jit(solution)/shard_map/while/body/eval_jaxpr/vqd,sd->vqs/dot_general | solution.py:21
  166.5 5.5 %convolution_reduce_fusion.2 = f32[16,32,64]{1,2,0:T(8,128)S(1)} fusion(bf16[64,64,128,1]{2,1,0,3:T(8,128)(2,1)S(1)} %bitcast.118, bf16[24,16,32,128]{3,2,1,0:T(8,128)(2,1)} %get-tuple-element.144, s32[]{:T(128)} %get-tuple-element.134), kind=kOutput, calls=%fused_computation.6.clone.1 | convolution fusion | flops 538935296 | bytes 1311232 | tf_op jit(solution)/shard_map/while/body/eval_jaxpr/vqd,sd->vqs/dot_general | solution.py:21
  172.7 5.5 %convolution_reduce_fusion.2 = f32[16,32,64]{1,2,0:T(8,128)S(1)} fusion(bf16[64,64,128,1]{2,1,0,3:T(8,128)(2,1)S(1)} %bitcast.118, bf16[24,16,32,128]{3,2,1,0:T(8,128)(2,1)} %get-tuple-element.144, s32[]{:T(128)} %get-tuple-element.134), kind=kOutput, calls=%fused_computation.6.clone.1 | convolution fusion | flops 538935296 | bytes 1311232 | tf_op jit(solution)/shard_map/while/body/eval_jaxpr/vqd,sd->vqs/dot_general | solution.py:21
  178.9 5.5 %convolution_reduce_fusion.2 = f32[16,32,64]{1,2,0:T(8,128)S(1)} fusion(bf16[64,64,128,1]{2,1,0,3:T(8,128)(2,1)S(1)} %bitcast.118, bf16[24,16,32,128]{3,2,1,0:T(8,128)(2,1)} %get-tuple-element.144, s32[]{:T(128)} %get-tuple-element.134), kind=kOutput, calls=%fused_computation.6.clone.1 | convolution fusion | flops 538935296 | bytes 1311232 | tf_op jit(solution)/shard_map/while/body/eval_jaxpr/vqd,sd->vqs/dot_general | solution.py:21
  185.0 5.5 %convolution_reduce_fusion.2 = f32[16,32,64]{1,2,0:T(8,128)S(1)} fusion(bf16[64,64,128,1]{2,1,0,3:T(8,128)(2,1)S(1)} %bitcast.118, bf16[24,16,32,128]{3,2,1,0:T(8,128)(2,1)} %get-tuple-element.144, s32[]{:T(128)} %get-tuple-element.134), kind=kOutput, calls=%fused_computation.6.clone.1 | convolution fusion | flops 538935296 | bytes 1311232 | tf_op jit(solution)/shard_map/while/body/eval_jaxpr/vqd,sd->vqs/dot_general | solution.py:21
  191.2 5.5 %convolution_reduce_fusion.2 = f32[16,32,64]{1,2,0:T(8,128)S(1)} fusion(bf16[64,64,128,1]{2,1,0,3:T(8,128)(2,1)S(1)} %bitcast.118, bf16[24,16,32,128]{3,2,1,0:T(8,128)(2,1)} %get-tuple-element.144, s32[]{:T(128)} %get-tuple-element.134), kind=kOutput, calls=%fused_computation.6.clone.1 | convolution fusion | flops 538935296 | bytes 1311232 | tf_op jit(solution)/shard_map/while/body/eval_jaxpr/vqd,sd->vqs/dot_general | solution.py:21
  197.4 5.5 %convolution_reduce_fusion.2 = f32[16,32,64]{1,2,0:T(8,128)S(1)} fusion(bf16[64,64,128,1]{2,1,0,3:T(8,128)(2,1)S(1)} %bitcast.118, bf16[24,16,32,128]{3,2,1,0:T(8,128)(2,1)} %get-tuple-element.144, s32[]{:T(128)} %get-tuple-element.134), kind=kOutput, calls=%fused_computation.6.clone.1 | convolution fusion | flops 538935296 | bytes 1311232 | tf_op jit(solution)/shard_map/while/body/eval_jaxpr/vqd,sd->vqs/dot_general | solution.py:21
  203.6 5.5 %convolution_reduce_fusion.2 = f32[16,32,64]{1,2,0:T(8,128)S(1)} fusion(bf16[64,64,128,1]{2,1,0,3:T(8,128)(2,1)S(1)} %bitcast.118, bf16[24,16,32,128]{3,2,1,0:T(8,128)(2,1)} %get-tuple-element.144, s32[]{:T(128)} %get-tuple-element.134), kind=kOutput, calls=%fused_computation.6.clone.1 | convolution fusion | flops 538935296 | bytes 1311232 | tf_op jit(solution)/shard_map/while/body/eval_jaxpr/vqd,sd->vqs/dot_general | solution.py:21
  209.7 5.5 %convolution_reduce_fusion.2 = f32[16,32,64]{1,2,0:T(8,128)S(1)} fusion(bf16[64,64,128,1]{2,1,0,3:T(8,128)(2,1)S(1)} %bitcast.118, bf16[24,16,32,128]{3,2,1,0:T(8,128)(2,1)} %get-tuple-element.144, s32[]{:T(128)} %get-tuple-element.134), kind=kOutput, calls=%fused_computation.6.clone.1 | convolution fusion | flops 538935296 | bytes 1311232 | tf_op jit(solution)/shard_map/while/body/eval_jaxpr/vqd,sd->vqs/dot_general | solution.py:21
  215.9 5.5 %convolution_reduce_fusion.2 = f32[16,32,64]{1,2,0:T(8,128)S(1)} fusion(bf16[64,64,128,1]{2,1,0,3:T(8,128)(2,1)S(1)} %bitcast.118, bf16[24,16,32,128]{3,2,1,0:T(8,128)(2,1)} %get-tuple-element.144, s32[]{:T(128)} %get-tuple-element.134), kind=kOutput, calls=%fused_computation.6.clone.1 | convolution fusion | flops 538935296 | bytes 1311232 | tf_op jit(solution)/shard_map/while/body/eval_jaxpr/vqd,sd->vqs/dot_general | solution.py:21
  222.1 5.5 %convolution_reduce_fusion.2 = f32[16,32,64]{1,2,0:T(8,128)S(1)} fusion(bf16[64,64,128,1]{2,1,0,3:T(8,128)(2,1)S(1)} %bitcast.118, bf16[24,16,32,128]{3,2,1,0:T(8,128)(2,1)} %get-tuple-element.144, s32[]{:T(128)} %get-tuple-element.134), kind=kOutput, calls=%fused_computation.6.clone.1 | convolution fusion | flops 538935296 | bytes 1311232 | tf_op jit(solution)/shard_map/while/body/eval_jaxpr/vqd,sd->vqs/dot_general | solution.py:21
  228.5 10.4 %all_to_all.15 = f32[32,1,240]{2,1,0:T(1,128)S(1)} all-to-all(f32[32,1,240]{2,1,0:T(1,128)S(1)} %reshape.144), channel_id=1, replica_groups=mesh['group'=4,'shard'=8] {'group','shard'}, dimensions={0} | all-to-all | bytes 61440 | tf_op jit(solution)/shard_map/all_to_all | solution.py:33
  239.4 0.7 reduce.69
  240.4 0.6 gather_fusion.3
  241.0 0.7 reshape.57
  (230 shorter events, 31.6 us)
Async XLA Ops:
  6.5 1.5 copy-start
  6.5 68.6 %all-gather.2.cloned.1.call-start = ((), (), s32[]{:S(2)}) async-start(), calls=%async_computation.3 | async-start | bytes 4325376 | tf_op jit(solution)/shard_map/all_gather | solution.py:59
  41.1 14.4 %all-to-all-start.1 = ((s32[32,12,1]{1,2,0:T(1,128)}), s32[32,12,1]{1,2,0:T(1,128)S(1)}, u32[]{:S(2)}, u32[]{:S(2)}) async-start(s32[32,12,1]{1,2,0:T(1,128)} %constant_dynamic-update-slice_fusion), calls=%async_computation.1 | async-start | bytes 32768 | tf_op jit(solution)/shard_map/all_to_all | solution.py:65
  55.5 10.0 %all-to-all-start = ((s32[32,1,240]{2,1,0:T(1,128)}), s32[32,1,240]{2,1,0:T(1,128)S(1)}, u32[]{:S(2)}, u32[]{:S(2)}) async-start(s32[32,1,240]{2,1,0:T(1,128)} %reshape.142), calls=%async_computation | async-start | bytes 65536 | tf_op jit(solution)/shard_map/all_to_all | solution.py:71
  66.9 13.2 %copy-start.1 = (bf16[64,64,128]{2,1,0:T(8,128)(2,1)S(1)}, bf16[64,64,128]{2,1,0:T(8,128)(2,1)}, u32[]{:S(2)}) copy-start(bf16[64,64,128]{2,1,0:T(8,128)(2,1)} %param.7) | copy-start | bytes 3145732
Sparse Core Ops, SparseCore 0:
  10.3 64.7 all-gather.1
